TPU v7x, 32 devices: a whole 2x2x4 slice. The times are simulated.
32 devices in a mesh: pix: 16 (over z, y, core), chan: 2 (over x).
Axes of the slice: x: 2, y: 2, z: 4, core: 2. Of those that a mesh axis runs over, the one named last changes fastest.
Arguments:
- spectra: float32 [32768, 4096], P('pix', 'chan'), may hold values from 0.1 to 3
- coeffs: float32 [32, 32768], P(None, 'pix'), may hold values from 0.05 to 0.5
- endmembers: float32 [32, 4096], P(None, 'chan'), may hold values from 0.05 to 0.5
- pixel_mask: int32 [32768], P('pix'), may hold values from 0 to 1
- labels: int32 [32768], P('pix'), may hold values from 0 to 23
Outputs:
- new_coeffs: float32 [32, 32768], P(None, 'pix')
- new_endmembers: float32 [32, 4096], P(None, 'chan')
- centroids: float32 [24, 4096], P(None, 'chan')
- distances: float32 [32768], P('pix')
All inputs are finite; a program needn't handle non-finite values.
Results may differ from a plain program's by a relative error of at most 0.0003.
Values sent between devices are 32-bit elements; how exact they have to be, the bound alone decides.
No kernel may reach another device: no remote copies, remote signals or barrier semaphores. Data moves between devices by JAX's collectives and lax.ppermute only.
A program may use at most 64 MiB of HBM per device.

v0:
```python
import jax
import jax.numpy as jnp
from jax import lax
from jax.sharding import PartitionSpec as P

PHASES = 24


EPSILON = 1e-06


def product(left, right):
    return jnp.dot(left, right, precision=lax.Precision.HIGHEST, preferred_element_type=jnp.float32)


def contract(left, right, left_dim, right_dim):
    return lax.dot_general(
        left,
        right,
        (((left_dim,), (right_dim,)), ((), ())),
        precision=lax.Precision.HIGHEST,
        preferred_element_type=jnp.float32,
    )


def local(spectra, coeffs, endmembers, pixel_mask, labels):
    channels_total = endmembers.shape[1] * lax.axis_size("chan")
    local_numer = contract(endmembers, spectra, 1, 1)
    local_gram = contract(endmembers, endmembers, 1, 1)
    numer_coeff, gram_all = lax.psum((local_numer, local_gram), "chan")
    new_coeffs = coeffs * numer_coeff / (product(gram_all, coeffs) + EPSILON)
    weights = pixel_mask.astype(jnp.float32)
    weighted = new_coeffs * weights[None, :]
    onehot = (labels[None, :] == jnp.arange(PHASES, dtype=jnp.int32)[:, None]).astype(jnp.float32)
    picked = onehot * weights[None, :]
    numer_end, outer_gram, phase_sums, phase_counts = lax.psum(
        (
            product(weighted, spectra),
            contract(weighted, new_coeffs, 1, 1),
            contract(picked, new_coeffs, 1, 1),
            jnp.sum(picked, axis=1),
        ),
        "pix",
    )
    new_endmembers = endmembers * numer_end / (product(outer_gram, endmembers) + EPSILON)
    phase_means = phase_sums / (phase_counts + 1.0)[:, None]
    centroids = product(phase_means, new_endmembers)
    gram_updated = lax.psum(contract(new_endmembers, new_endmembers, 1, 1), "chan")
    offset = new_coeffs - contract(phase_means, onehot, 0, 0)
    distance = jnp.sum(offset * product(gram_updated, offset), axis=0) / channels_total
    return (new_coeffs, new_endmembers, centroids, distance)


def solution(mesh):
    placed = (P("pix", "chan"), P(None, "pix"), P(None, "chan"), P("pix"), P("pix"))
    return jax.shard_map(
        local,
        mesh=mesh,
        in_specs=placed,
        out_specs=(P(None, "pix"), P(None, "chan"), P(None, "chan"), P("pix")),
        check_vma=False,
    )
```

profile of v0, /device:TPU:0, one launch (start us, length us, event | category | flops | bytes accessed | tf_op | source)
XLA Modules:
  0.0 179.4 jit_solution(9026116440240854238)
XLA Ops:
  7.2 0.0 all-reduce.4.cloned.1.call-start
  7.3 21.4 %fusion.17 = f32[32,2048]{1,0:T(8,128)} fusion(f32[32,2048]{1,0:T(8,128)} %param.7, f32[2048,2048]{1,0:T(8,128)} %param.5), kind=kOutput, calls=%fused_computation.26 | convolution fusion | flops 1610612736 | bytes 17301504 | tf_op jit(solution)/shard_map/dot_general | solution.py:17
  28.6 0.0 all-reduce.4.cloned.1.call-update
  28.7 0.0 all-reduce.6.cloned.1.call-start
  28.7 0.4 fusion.18
  29.1 9.7 %psum.50 = f32[32,32]{1,0:T(8,128)S(1)} all-reduce(f32[32,32]{1,0:T(8,128)S(1)} %fusion.18), channel_id=1, replica_groups=mesh['pix'=16,'chan'=2] {'chan'}, use_global_device_ids=true, to_apply=%region_1.0 | all-reduce | flops 1024 | bytes 8192 | tf_op jit(solution)/shard_map/psum | solution.py:30
  38.8 0.1 select_reduce_fusion
  38.9 16.0 %all-reduce.4.cloned.1.call-done = f32[32,2048]{1,0:T(8,128)} async-done(((f32[32,2048]{1,0:T(8,128)}), f32[32,2048]{1,0:T(8,128)}) %all-reduce.4.cloned.1.call-update) | async-done | bytes 262160 | tf_op jit(solution)/shard_map/psum | solution.py:30
  54.9 1.3 fusion.1
  56.3 0.0 copy-start
  56.3 0.3 fusion.3
  56.6 0.3 fusion.7
  56.9 13.9 %fusion.5 = f32[32,2048]{1,0:T(8,128)} fusion(f32[2048,2048]{1,0:T(8,128)} %param.5, f32[32,2048]{1,0:T(8,128)S(1)} %fusion.1, f32[2048]{0:T(1024)S(1)} %convert_element_type.4), kind=kOutput, calls=%fused_computation.9 | convolution fusion | flops 1610678272 | bytes 17309696 | tf_op jit(solution)/shard_map/dot_general | solution.py:13
  70.8 0.0 all-reduce.6.cloned.1.call-update
  70.8 60.7 %all-reduce = (f32[32,32]{1,0:T(8,128)S(1)}, f32[24,32]{1,0:T(8,128)S(1)}, f32[24]{0:T(128)S(1)}) all-reduce(f32[32,32]{1,0:T(8,128)S(1)} %fusion.3, f32[24,32]{1,0:T(8,128)S(1)} %fusion.7, f32[24]{0:T(128)S(1)} %select_reduce_fusion), channel_id=1, replica_groups=mesh['pix'=16,'chan'=2] {'pix'}, use_global_device_ids=true, to_apply=%region_3.0 | all-reduce | flops 1816 | bytes 14528 | tf_op jit(solution)/shard_map/psum | solution.py:36
  131.5 0.4 convolution_subtract_fusion
  131.9 28.7 %all-reduce.6.cloned.1.call-done = f32[32,2048]{1,0:T(8,128)} async-done(((f32[32,2048]{1,0:T(8,128)}), f32[32,2048]{1,0:T(8,128)}) %all-reduce.6.cloned.1.call-update) | async-done | bytes 262160 | tf_op jit(solution)/shard_map/psum | solution.py:36
  160.7 1.3 fusion
  162.0 0.0 copy-start.2
  162.0 1.1 fusion.15
  163.1 0.4 fusion.19
  163.4 8.1 %psum.55 = f32[32,32]{1,0:T(8,128)S(1)} all-reduce(f32[32,32]{1,0:T(8,128)S(1)} %fusion.19), channel_id=1, replica_groups=mesh['pix'=16,'chan'=2] {'chan'}, use_global_device_ids=true, to_apply=%region_7.0 | all-reduce | flops 1024 | bytes 8192 | tf_op jit(solution)/shard_map/psum | solution.py:48
  171.5 0.4 fusion.2
  171.9 0.6 broadcast_multiply_fusion
  (12 shorter events, 0.0 us)
Async XLA Ops:
  7.2 21.6 %copy-start.1 = (f32[32,2048]{1,0:T(8,128)S(1)}, f32[32,2048]{1,0:T(8,128)}, u32[]{:S(2)}) copy-start(f32[32,2048]{1,0:T(8,128)} %param.7) | copy-start | bytes 786436
  7.2 21.5 %copy-start.4 = (s32[2048]{0:T(1024)S(1)}, s32[2048]{0:T(1024)}, u32[]{:S(2)}) copy-start(s32[2048]{0:T(1024)} %param.8) | copy-start | bytes 24580
  7.2 31.6 %copy-start.3 = (s32[2048]{0:T(1024)S(1)}, s32[2048]{0:T(1024)}, u32[]{:S(2)}) copy-start(s32[2048]{0:T(1024)} %param.9) | copy-start | bytes 24580
  7.2 47.7 %copy-start.5 = (f32[32,2048]{1,0:T(8,128)S(1)}, f32[32,2048]{1,0:T(8,128)}, u32[]{:S(2)}) copy-start(f32[32,2048]{1,0:T(8,128)} %param.6) | copy-start | bytes 786436
  7.2 47.7 %all-reduce.4.cloned.1.call-start = ((), (), s32[]{:S(2)}) async-start(), calls=%async_computation | async-start | bytes 524288 | tf_op jit(solution)/shard_map/psum | solution.py:30
  28.7 132.0 %all-reduce.6.cloned.1.call-start = ((), (), s32[]{:S(2)}) async-start(), calls=%async_computation.1 | async-start | bytes 524288 | tf_op jit(solution)/shard_map/psum | solution.py:36
  56.3 116.3 %copy-start = (f32[32,2048]{1,0:T(8,128)}, f32[32,2048]{1,0:T(8,128)S(1)}, u32[]{:S(2)}) copy-start(f32[32,2048]{1,0:T(8,128)S(1)} %fusion.1) | copy-start | bytes 786436
  162.0 10.5 %copy-start.2 = (f32[32,2048]{1,0:T(8,128)}, f32[32,2048]{1,0:T(8,128)S(1)}, u32[]{:S(2)}) copy-start(f32[32,2048]{1,0:T(8,128)S(1)} %fusion) | copy-start | bytes 786436
Sparse Core Ops, SparseCore 0:
  28.8 26.0 all-reduce.3
  70.9 89.7 all-reduce.5
where the time goes:
time: 180 us; the launch traced here: 179 us
  blocking collectives  78.5 us (44%)
  waiting for transfers between devices  44.8 us (25%)
  matrix products  41 us (23%)
  between operations  14.2 us (8%)
    psum x1, blocking collectives, local(): lax.psum((product(weighted, spectra), contract(weighted, new_coeffs, 1, 1...  60.7 us
    psum x1, waiting for transfers between devices, local(): lax.psum((product(weighted, spectra), contract(weighted, new_coeffs, 1, 1...  28.7 us
    dot_general x6, matrix products, contract(): lax.dot_general(left, right, (((left_dim,), (right_dim,)), ((), ())), pre...  23.1 us
    dot_general x5, matrix products, product(): jnp.dot(left, right, precision=lax.Precision.HIGHEST, preferred_element_t...  17.9 us
    psum x1, waiting for transfers between devices, local(): numer_coeff, gram_all = lax.psum((local_numer, local_gram), 'chan')  16 us
    psum x1, blocking collectives, local(): numer_coeff, gram_all = lax.psum((local_numer, local_gram), 'chan')  9.69 us
    psum x1, blocking collectives, local(): lax.psum(contract(new_endmembers, new_endmembers, 1, 1), 'chan')  8.11 us
  transfers between devices with their start and end apart: 2, of which 2 were waited for; matrix products, arithmetic and copies ran while one was open for 1% of the time, Pallas kernels for 0%

commit v1 on v0

v1 whole, which is shorter than its diff:
```python
import jax
import jax.numpy as jnp
from jax import lax
from jax.experimental import pallas as pl
from jax.experimental.pallas import tpu as pltpu
from jax.sharding import PartitionSpec as P


PHASES = 24
EPSILON = 1e-06
TILE = 128
AHEAD = 4
CORE, NEAR, FAR = 1, 2, 4


F32 = jnp.float32
BF16 = jnp.bfloat16
VMEM = pl.BlockSpec(memory_space=pltpu.VMEM)
HBM = pl.BlockSpec(memory_space=pl.ANY)


def dot(left, right, left_dim, right_dim):
    return lax.dot_general(
        left,
        right,
        (((left_dim,), (right_dim,)), ((), ())),
        precision=lax.Precision.HIGHEST,
        preferred_element_type=F32,
    )


def dot_bf16(left, right, left_dim, right_dim):
    return lax.dot_general(
        left, right, (((left_dim,), (right_dim,)), ((), ())), preferred_element_type=F32
    )


def split(value):
    high = value.astype(BF16)
    low = (value - high.astype(F32)).astype(BF16)
    return high, low


def stacked(value):
    return jnp.concatenate(split(value), axis=0)


def in_vmem(value):
    return pltpu.with_memory_space_constraint(value, pltpu.VMEM)


def in_hbm(value):
    return pltpu.with_memory_space_constraint(value, pltpu.HBM)


def columns_per_block(channels):
    return 256 if channels % 256 == 0 else channels


def numerator(spectra, endmembers, first, rows, with_gram):
    channels = spectra.shape[1]
    members = endmembers.shape[0]
    step = columns_per_block(channels)
    count = channels // step
    extra = TILE if with_gram else 0

    def kernel(ends_hbm, spectra_hbm, out_ref, high_ref, low_ref, ends_ref, buffer, sems):
        copies = [
            pltpu.make_async_copy(
                spectra_hbm.at[pl.ds(first, rows), pl.ds(i * step, step)], buffer.at[i % AHEAD], sems.at[i]
            )
            for i in range(count)
        ]
        ends_copy = pltpu.make_async_copy(ends_hbm, ends_ref, sems.at[count])
        ends_copy.start()
        for i in range(min(AHEAD, count)):
            copies[i].start()
        ends_copy.wait()
        ends = stacked(ends_ref[...])
        if with_gram:
            gram = dot_bf16(ends, ends, 1, 1)
            gram = gram[:members] + gram[members:]
            gram = gram[:, :members] + gram[:, members:]
            out_ref[:, rows:] = jnp.concatenate(
                [gram, jnp.zeros((members, TILE - members), F32)], axis=1
            )
        total = None
        for i in range(count):
            copies[i].wait()
            high, low = split(buffer[i % AHEAD])
            if i + AHEAD < count:
                copies[i + AHEAD].start()
            high_ref[:, i * step : (i + 1) * step] = high
            low_ref[:, i * step : (i + 1) * step] = low
            left = ends[:, i * step : (i + 1) * step]
            part = dot_bf16(left, high, 1, 1) + dot_bf16(left, low, 1, 1)
            total = part if total is None else total + part
        out_ref[:, :rows] = total[:members] + total[members:]

    return pl.pallas_call(
        kernel,
        in_specs=[HBM, HBM],
        out_specs=[VMEM] * 3,
        out_shape=[
            jax.ShapeDtypeStruct((members, rows + extra), F32),
            pltpu.VMEM((rows, channels), BF16),
            pltpu.VMEM((rows, channels), BF16),
        ],
        scratch_shapes=[
            pltpu.VMEM((members, channels), F32),
            pltpu.VMEM((AHEAD, rows, step), F32),
            pltpu.SemaphoreType.DMA((count + 1,)),
        ],
        compiler_params=pltpu.CompilerParams(vmem_limit_bytes=20 << 20),
        cost_estimate=pl.CostEstimate(
            flops=8 * members * rows * channels, bytes_accessed=8 * rows * channels, transcendentals=0
        ),
        name="numerator",
    )(in_hbm(endmembers), in_hbm(spectra))


def update(high, low, sums, gram, coeffs, mask, labels, before=()):
    members, pixels = coeffs.shape
    channels = high.shape[1]

    def kernel(high_ref, low_ref, sums_ref, gram_ref, coeffs_ref, mask_ref, labels_ref, *refs):
        new_ref, tile_ref, end_ref = refs[-3:]
        old = coeffs_ref[...]
        new = old * sums_ref[...] / (dot(gram_ref[...], old, 1, 0) + EPSILON)
        new_ref[...] = new
        weight = mask_ref[...].astype(F32)
        weighted = new * weight
        terms = stacked(weighted)
        phase = lax.broadcasted_iota(jnp.int32, (members, pixels), 0)
        picked = jnp.where(phase == labels_ref[...], weight, 0.0)
        counts = jnp.sum(picked, axis=1, keepdims=True)
        both = dot(jnp.concatenate([weighted, picked], axis=0), new, 1, 1)
        tile = jnp.concatenate(
            [both[:members], both[members:], jnp.broadcast_to(counts, (members, TILE - 2 * members))], axis=1
        )
        left = jnp.concatenate([terms, terms], axis=1)
        right = jnp.concatenate([high_ref[...], low_ref[...]], axis=0)
        part = dot_bf16(left, right, 1, 0)
        end = part[:members] + part[members:]
        if before:
            tile = tile + refs[0][...]
            end = end + refs[1][...]
        tile_ref[...] = tile
        end_ref[...] = end

    return pl.pallas_call(
        kernel,
        in_specs=[VMEM] * (7 + len(before)),
        out_specs=[VMEM] * 3,
        out_shape=[
            jax.ShapeDtypeStruct((members, pixels), F32),
            jax.ShapeDtypeStruct((members, TILE), F32),
            jax.ShapeDtypeStruct((members, channels), F32),
        ],
        compiler_params=pltpu.CompilerParams(vmem_limit_bytes=16 << 20),
        cost_estimate=pl.CostEstimate(
            flops=8 * members * pixels * channels, bytes_accessed=4 * pixels * channels, transcendentals=0
        ),
        name="update",
    )(in_vmem(high), in_vmem(low), sums, gram, coeffs, mask, labels, *before)


def partner(value, axis, bit):
    pairs = [(i, i ^ bit) for i in range(lax.axis_size(axis))]
    return lax.ppermute(value, axis, pairs)


def bits(axis, first=1):
    size = lax.axis_size(axis)
    if size & (size - 1):
        raise ValueError("axis size")
    found = []
    while first < size:
        found.append(first)
        first *= 2
    return found


def summed(value, axis, order):
    for bit in order:
        value = value + partner(value, axis, bit)
    return value


def across(value, bit):
    pix, chan = lax.axis_size("pix"), lax.axis_size("chan")
    pairs = [
        (i * chan + j, (i ^ bit) * chan + (j ^ 1)) for i in range(pix) for j in range(chan)
    ]
    return lax.ppermute(value, ("pix", "chan"), pairs)


def halved(value, low):
    width = value.shape[1] // 2
    left, right = value[:, :width], value[:, width:]
    return jnp.where(low, left, right), jnp.where(low, right, left)


def joined(mine, other, low):
    return jnp.concatenate([jnp.where(low, mine, other), jnp.where(low, other, mine)], axis=1)


def beside(*values):
    return jnp.concatenate(values, axis=1)


def local(spectra, coeffs, endmembers, pixel_mask, labels):
    pixels, channels = spectra.shape
    members = coeffs.shape[0]
    channels_total = channels * lax.axis_size("chan")
    chan_bits = bits("chan")
    half = pixels // 2
    mask_row, label_row = pixel_mask[None, :], labels[None, :]

    index = lax.axis_index("pix")
    core_low = jnp.bitwise_and(index, CORE) == 0
    near_low = jnp.bitwise_and(index, NEAR) == 0
    endmembers, core_low, near_low = lax.optimization_barrier((endmembers, core_low, near_low))

    sums_a, high_a, low_a = numerator(spectra, endmembers, 0, half, True)
    sums_b, high_b, low_b = numerator(spectra, endmembers, half, half, False)
    sums_a = summed(sums_a, "chan", chan_bits)
    sums_b = summed(sums_b, "chan", chan_bits)
    gram = sums_a[:, half : half + members]
    new_a, tile_a, end_a = update(
        high_a, low_a, sums_a[:, :half], gram, coeffs[:, :half], mask_row[:, :half], label_row[:, :half]
    )
    new_b, tile, end = update(
        high_b, low_b, sums_b, gram, coeffs[:, half:], mask_row[:, half:], label_row[:, half:], (tile_a, end_a)
    )
    new_coeffs = beside(new_a, new_b)

    mine, other = halved(end, core_low)
    total = beside(mine, tile) + partner(beside(other, tile), "pix", CORE)
    width = mine.shape[1]
    mine, other = halved(total[:, :width], near_low)
    tile = total[:, width:]
    total = beside(mine, tile) + partner(beside(other, tile), "pix", NEAR)
    total = summed(total, "pix", bits("pix", FAR))
    width = mine.shape[1]
    outer_gram = total[:, width : width + members]
    phase_sums = total[:PHASES, width + members : width + 2 * members]
    phase_counts = total[:PHASES, width + 2 * members : width + 2 * members + 1]

    ends = halved(halved(endmembers, core_low)[0], near_low)[0]
    new = ends * total[:, :width] / (dot(outer_gram, ends, 1, 0) + EPSILON)
    gram_new = dot(new, new, 1, 1)
    padding = jnp.zeros((members, TILE - members), F32)
    got = partner(beside(new, gram_new, padding), "pix", NEAR)
    from_chan = partner(gram_new, "chan", 1)
    from_both = across(gram_new, NEAR)
    gram_new = gram_new + from_chan + from_both + got[:, width : width + members]
    new = joined(new, got[:, :width], near_low)
    gram_new = summed(gram_new, "chan", chan_bits[1:])
    new_endmembers = joined(new, partner(new, "pix", CORE), core_low)
    gram_new = gram_new + partner(gram_new, "pix", CORE)
    phase_means = phase_sums / (phase_counts + 1.0)
    centroids = dot(phase_means, new_endmembers, 1, 0)
    onehot = (labels[None, :] == jnp.arange(PHASES, dtype=jnp.int32)[:, None]).astype(F32)
    offset = new_coeffs - dot(phase_means, onehot, 0, 0)
    distance = jnp.sum(offset * dot(gram_new / channels_total, offset, 1, 0), axis=0)
    return (new_coeffs, new_endmembers, centroids, distance)


def solution(mesh):
    placed = (P("pix", "chan"), P(None, "pix"), P(None, "chan"), P("pix"), P("pix"))
    return jax.shard_map(
        local,
        mesh=mesh,
        in_specs=placed,
        out_specs=(P(None, "pix"), P(None, "chan"), P(None, "chan"), P("pix")),
        check_vma=False,
    )
```

time: 180 us -> 50.4 us (0.28)
  blocking collectives: 78.5 us -> 0 us
  matrix products: 41 us -> 2.81 us
  waiting for transfers between devices: 44.8 us -> 18.6 us
  Pallas kernels: 0 us -> 14 us
  between operations: 14.2 us -> 0.93 us
  starting transfers between devices: 0.08 us -> 13.2 us
    psum x3 -> x0, blocking collectives: 78.5 us -> none  [the longest x1 60.7 us: local(): lax.psum((product(weighted, spectra), contract(weighted, new_coeffs, 1, 1...]
    psum x2 -> x0, waiting for transfers between devices: 44.7 us -> none  [the longest x1 28.7 us: local(): lax.psum((product(weighted, spectra), contract(weighted, new_coeffs, 1, 1...]
    dot_general x11 -> x5, matrix products: 41 us -> 2.81 us  [dot(): lax.dot_general(left, right, (((left_dim,), (right_dim,)), ((), ())), pre...]
    ppermute x0 -> x11, waiting for transfers between devices: none -> 18.6 us  [the longest x10 17.4 us: partner(): return lax.ppermute(value, axis, pairs)]
    pallas_call x0 -> x4, Pallas kernels: none -> 14 us  [the longest x2 10.2 us: numerator(): pl.pallas_call(kernel, in_specs=[HBM, HBM], out_specs=[VMEM] * 3, out_sha...]
    ppermute x0 -> x11, starting transfers between devices: none -> 13.2 us  [the longest x10 10.6 us: partner(): return lax.ppermute(value, axis, pairs)]
  transfers between devices with their start and end apart: 2 -> 11, of which waited for: 2 -> 8; matrix products, arithmetic and copies ran while one was open for 1% -> 3% of each run, Pallas kernels for 0% -> 9%
where the time goes in v1:
time: 50.4 us; the launch traced here: 50.2 us
  waiting for transfers between devices  18.6 us (37%)
  Pallas kernels  14 us (28%)
  starting transfers between devices  13.2 us (26%)
  matrix products  2.81 us (6%)
  between operations  0.93 us (2%)
    ppermute x10, waiting for transfers between devices, partner(): return lax.ppermute(value, axis, pairs)  17.4 us
    ppermute x10, starting transfers between devices, partner(): return lax.ppermute(value, axis, pairs)  10.6 us
    pallas_call x2, Pallas kernels, numerator(): pl.pallas_call(kernel, in_specs=[HBM, HBM], out_specs=[VMEM] * 3, out_sha...  10.2 us
    pallas_call x2, Pallas kernels, update(): pl.pallas_call(kernel, in_specs=[VMEM] * (7 + len(before)), out_specs=[VM...  3.83 us
    dot_general x5, matrix products, dot(): lax.dot_general(left, right, (((left_dim,), (right_dim,)), ((), ())), pre...  2.81 us
    ppermute x1, starting transfers between devices, across(): return lax.ppermute(value, ('pix', 'chan'), pairs)  2.67 us
    ppermute x1, waiting for transfers between devices, across(): return lax.ppermute(value, ('pix', 'chan'), pairs)  1.2 us
  transfers between devices with their start and end apart: 11, of which 8 were waited for; matrix products, arithmetic and copies ran while one was open for 3% of the time, Pallas kernels for 9%

profile of v1, /device:TPU:0, one launch (start us, length us, event | category | flops | bytes accessed | tf_op | source)
XLA Modules:
  0.0 50.2 jit_solution(12736798321006048066)
XLA Ops:
  0.6 5.6 %numerator.2 = (f32[32,1152]{1,0:T(8,128)S(1)}, bf16[1024,2048]{1,0:T(8,128)(2,1)S(1)}, bf16[1024,2048]{1,0:T(8,128)(2,1)S(1)}) custom-call(f32[32,2048]{1,0:T(8,128)} %ends_hbm.1, f32[2048,2048]{1,0:T(8,128)} %spectra_hbm.3), custom_call_target="tpu_custom_call" | custom-call | flops 536870912 | bytes 16777216 | tf_op jit(solution)/shard_map/numerator/pallas_call | solution.py:100
  6.3 3.0 %collective-permute-start = (f32[32,1152]{1,0:T(8,128)S(1)}, f32[32,1152]{1,0:T(8,128)S(1)}, u32[]{:S(2)}, u32[]{:S(2)}) collective-permute-start(f32[32,1152]{1,0:T(8,128)S(1)} %get-tuple-element.22), channel_id=1, source_target_pairs={{0,1},{1,0},{2,3},{3,2},{4,5},{5,4},{6,7},{7,6},{8,9},{9,8},{10,11... | collective-permute-start | bytes 442376 | tf_op jit(solution)/shard_map/ppermute | solution.py:170
  9.3 4.6 %numerator.3 = (f32[32,1024]{1,0:T(8,128)S(1)}, bf16[1024,2048]{1,0:T(8,128)(2,1)S(1)}, bf16[1024,2048]{1,0:T(8,128)(2,1)S(1)}) custom-call(f32[32,2048]{1,0:T(8,128)} %ends_hbm.1, f32[2048,2048]{1,0:T(8,128)} %spectra_hbm.3), custom_call_target="tpu_custom_call" | custom-call | flops 536870912 | bytes 16777216 | tf_op jit(solution)/shard_map/numerator/pallas_call | solution.py:100
  14.1 4.9 %collective-permute-done.1 = f32[32,1024]{1,0:T(8,128)S(1)} collective-permute-done((f32[32,1024]{1,0:T(8,128)S(1)}, f32[32,1024]{1,0:T(8,128)S(1)}, u32[]{:S(2)}, u32[]{:S(2)}) %collective-permute-start.1) | collective-permute-done | bytes 131104 | tf_op jit(solution)/shard_map/ppermute | solution.py:170
  19.0 1.9 %update.2 = (f32[32,1024]{1,0:T(8,128)S(1)}, f32[32,128]{1,0:T(8,128)S(1)}, f32[32,2048]{1,0:T(8,128)S(1)}) custom-call(bf16[1024,2048]{1,0:T(8,128)(2,1)S(1)} %get-tuple-element.20.high_ref, bf16[1024,2048]{1,0:T(8,128)(2,1)S(1)} %get-tuple-element.21.low_ref, f32[32,1024]{1,0:T(8,128)S(1)} %slice.95.sums_ref, f32[32,32]{1,0:T(8,128)S(1)} %slice.96.gram_ref, ...), custom_call_target="tpu_custom_call" | custom-call | flops 536870912 | bytes 8388608 | tf_op jit(solution)/shard_map/update/pallas_call | solution.py:151
  21.0 1.9 %update.3 = (f32[32,1024]{1,0:T(8,128)S(1)}, f32[32,128]{1,0:T(8,128)S(1)}, f32[32,2048]{1,0:T(8,128)S(1)}) custom-call(bf16[1024,2048]{1,0:T(8,128)(2,1)S(1)} %get-tuple-element.24.high_ref, bf16[1024,2048]{1,0:T(8,128)(2,1)S(1)} %get-tuple-element.25.low_ref, f32[32,1024]{1,0:T(8,128)S(1)} %add.40.sums_ref, f32[32,32]{1,0:T(8,128)S(1)} %slice.96.gram_ref, ...), custom_call_target="tpu_custom_call" | custom-call | flops 536870912 | bytes 8388608 | tf_op jit(solution)/shard_map/update/pallas_call | solution.py:151
  23.0 1.4 %collective-permute-done.2 = f32[32,1152]{1,0:T(8,128)S(1)} collective-permute-done((f32[32,1152]{1,0:T(8,128)S(1)}, f32[32,1152]{1,0:T(8,128)S(1)}, u32[]{:S(2)}, u32[]{:S(2)}) %collective-permute-start.2) | collective-permute-done | bytes 147488 | tf_op jit(solution)/shard_map/ppermute | solution.py:170
  24.5 1.6 %collective-permute-start.3 = (f32[32,640]{1,0:T(8,128)S(1)}, f32[32,640]{1,0:T(8,128)S(1)}, u32[]{:S(2)}, u32[]{:S(2)}) collective-permute-start(f32[32,640]{1,0:T(8,128)S(1)} %pad_maximum_fusion.4), channel_id=1, source_target_pairs={{0,4},{2,6},{4,0},{6,2},{8,12},{10,14},{12,8},{14,10},{16,20},{18,... | collective-permute-start | bytes 245768 | tf_op jit(solution)/shard_map/ppermute | solution.py:170
  26.2 2.9 %collective-permute-done.3 = f32[32,640]{1,0:T(8,128)S(1)} collective-permute-done((f32[32,640]{1,0:T(8,128)S(1)}, f32[32,640]{1,0:T(8,128)S(1)}, u32[]{:S(2)}, u32[]{:S(2)}) %collective-permute-start.3) | collective-permute-done | bytes 81952 | tf_op jit(solution)/shard_map/ppermute | solution.py:170
  29.0 1.6 %collective-permute-start.4 = (f32[32,640]{1,0:T(8,128)S(1)}, f32[32,640]{1,0:T(8,128)S(1)}, u32[]{:S(2)}, u32[]{:S(2)}) collective-permute-start(f32[32,640]{1,0:T(8,128)S(1)} %fusion.3), channel_id=1, source_target_pairs={{0,8},{2,10},{4,12},{6,14},{8,0},{10,2},{12,4},{14,6},{16,24},{18,... | collective-permute-start | bytes 245768 | tf_op jit(solution)/shard_map/ppermute | solution.py:170
  30.7 2.9 %collective-permute-done.4 = f32[32,640]{1,0:T(8,128)S(1)} collective-permute-done((f32[32,640]{1,0:T(8,128)S(1)}, f32[32,640]{1,0:T(8,128)S(1)}, u32[]{:S(2)}, u32[]{:S(2)}) %collective-permute-start.4) | collective-permute-done | bytes 81952 | tf_op jit(solution)/shard_map/ppermute | solution.py:170
  33.6 2.7 %collective-permute-start.5 = (f32[32,640]{1,0:T(8,128)S(1)}, f32[32,640]{1,0:T(8,128)S(1)}, u32[]{:S(2)}, u32[]{:S(2)}) collective-permute-start(f32[32,640]{1,0:T(8,128)S(1)} %add.43), channel_id=1, source_target_pairs={{0,16},{2,18},{4,20},{6,22},{8,24},{10,26},{12,28},{14,30},{16,0},... | collective-permute-start | bytes 245768 | tf_op jit(solution)/shard_map/ppermute | solution.py:170
  36.2 2.7 %collective-permute-done.5 = f32[32,640]{1,0:T(8,128)S(1)} collective-permute-done((f32[32,640]{1,0:T(8,128)S(1)}, f32[32,640]{1,0:T(8,128)S(1)}, u32[]{:S(2)}, u32[]{:S(2)}) %collective-permute-start.5) | collective-permute-done | bytes 81952 | tf_op jit(solution)/shard_map/ppermute | solution.py:170
  39.0 0.2 fusion.4
  39.2 0.2 fusion.16
  39.4 0.4 collective-permute-start.8
  39.8 2.7 %collective-permute-start.9 = (f32[32,32]{1,0:T(8,128)S(1)}, f32[32,32]{1,0:T(8,128)S(1)}, u32[]{:S(2)}, u32[]{:S(2)}) collective-permute-start(f32[32,32]{1,0:T(8,128)S(1)} %fusion.16), channel_id=1, source_target_pairs={{0,5},{1,4},{2,7},{3,6},{4,1},{5,0},{6,3},{7,2},{8,13},{9,12},{10,... | collective-permute-start | bytes 12296 | tf_op jit(solution)/shard_map/ppermute | solution.py:195
  42.4 0.6 %collective-permute-start.6 = (f32[32,640]{1,0:T(8,128)S(1)}, f32[32,640]{1,0:T(8,128)S(1)}, u32[]{:S(2)}, u32[]{:S(2)}) collective-permute-start(f32[32,640]{1,0:T(8,128)S(1)} %maximum_maximum_fusion), channel_id=1, source_target_pairs={{0,4},{2,6},{4,0},{6,2},{8,12},{10,14},{12,8},{14,10},{16,20},{18,... | collective-permute-start | bytes 245768 | tf_op jit(solution)/shard_map/ppermute | solution.py:170
  43.2 1.2 %collective-permute-done.9 = f32[32,32]{1,0:T(8,128)S(1)} collective-permute-done((f32[32,32]{1,0:T(8,128)S(1)}, f32[32,32]{1,0:T(8,128)S(1)}, u32[]{:S(2)}, u32[]{:S(2)}) %collective-permute-start.9) | collective-permute-done | bytes 4128 | tf_op jit(solution)/shard_map/ppermute | solution.py:195
  44.4 2.5 %collective-permute-done.6 = f32[32,640]{1,0:T(8,128)S(1)} collective-permute-done((f32[32,640]{1,0:T(8,128)S(1)}, f32[32,640]{1,0:T(8,128)S(1)}, u32[]{:S(2)}, u32[]{:S(2)}) %collective-permute-start.6) | collective-permute-done | bytes 81952 | tf_op jit(solution)/shard_map/ppermute | solution.py:170
  47.0 0.6 %collective-permute-start.7 = (f32[32,1024]{1,0:T(8,128)S(1)}, f32[32,1024]{1,0:T(8,128)S(1)}, u32[]{:S(2)}, u32[]{:S(2)}) collective-permute-start(f32[32,1024]{1,0:T(8,128)S(1)} %pad_maximum_fusion.3), channel_id=1, source_target_pairs={{0,2},{2,0},{4,6},{6,4},{8,10},{10,8},{12,14},{14,12},{16,18},{18,... | collective-permute-start | bytes 393224 | tf_op jit(solution)/shard_map/ppermute | solution.py:170
  47.6 0.4 convolution_subtract_fusion
  48.1 1.0 %fusion = f32[2048]{0:T(1024)} fusion(f32[32,2048]{1,0:T(8,128)S(1)} %convolution_subtract_fusion, f32[32,32]{1,0:T(8,128)S(1)} %slice_add_fusion, f32[32,32]{1,0:T(8,128)S(1)} %collective-permute-done.10), kind=kOutput, calls=%fused_computation.2 | convolution fusion | flops 25296896 | bytes 278528 | tf_op jit(solution)/shard_map/dot_general | solution.py:23
  49.2 1.1 %fusion.11 = f32[24,2048]{1,0:T(8,128)} fusion(f32[32,2048]{1,0:T(8,128)S(1)} %pad_maximum_fusion, f32[32,640]{1,0:T(8,128)S(1)} %add.44, f32[24]{0:T(128)S(1)} %fusion.9), kind=kOutput, calls=%fused_computation.38 | convolution fusion | flops 18875136 | bytes 471552 | tf_op jit(solution)/shard_map/dot_general | solution.py:23
  (46 shorter events, 1.0 us)
Async XLA Ops:
  6.2 7.8 %copy-start.3 = (f32[32,2048]{1,0:T(8,128)S(1)}, f32[32,2048]{1,0:T(8,128)}, u32[]{:S(2)}) copy-start(f32[32,2048]{1,0:T(8,128)} %param.6) | copy-start | bytes 786436
  6.3 7.8 %copy-start.4 = (s32[2048]{0:T(1024)S(1)}, s32[2048]{0:T(1024)}, u32[]{:S(2)}) copy-start(s32[2048]{0:T(1024)} %param.9) | copy-start | bytes 24580
  6.3 7.8 %copy-start.5 = (s32[2048]{0:T(1024)S(1)}, s32[2048]{0:T(1024)}, u32[]{:S(2)}) copy-start(s32[2048]{0:T(1024)} %param.8) | copy-start | bytes 24580
  6.3 12.7 %collective-permute-start = (f32[32,1152]{1,0:T(8,128)S(1)}, f32[32,1152]{1,0:T(8,128)S(1)}, u32[]{:S(2)}, u32[]{:S(2)}) collective-permute-start(f32[32,1152]{1,0:T(8,128)S(1)} %get-tuple-element.22), channel_id=1, source_target_pairs={{0,1},{1,0},{2,3},{3,2},{4,5},{5,4},{6,7},{7,6},{8,9},{9,8},{10,11... | collective-permute-start | bytes 442376 | tf_op jit(solution)/shard_map/ppermute | solution.py:170
  13.9 5.0 %collective-permute-start.1 = (f32[32,1024]{1,0:T(8,128)S(1)}, f32[32,1024]{1,0:T(8,128)S(1)}, u32[]{:S(2)}, u32[]{:S(2)}) collective-permute-start(f32[32,1024]{1,0:T(8,128)S(1)} %get-tuple-element.26), channel_id=1, source_target_pairs={{0,1},{1,0},{2,3},{3,2},{4,5},{5,4},{6,7},{7,6},{8,9},{9,8},{10,11... | collective-permute-start | bytes 393224 | tf_op jit(solution)/shard_map/ppermute | solution.py:170
  21.0 5.1 %copy-start = (f32[32,2048]{1,0:T(8,128)S(1)}, f32[32,2048]{1,0:T(8,128)}, u32[]{:S(2)}) copy-start(f32[32,2048]{1,0:T(8,128)} %ends_hbm.1) | copy-start | bytes 786436
  23.0 1.4 %collective-permute-start.2 = (f32[32,1152]{1,0:T(8,128)S(1)}, f32[32,1152]{1,0:T(8,128)S(1)}, u32[]{:S(2)}, u32[]{:S(2)}) collective-permute-start(f32[32,1152]{1,0:T(8,128)S(1)} %pad_maximum_fusion.1), channel_id=1, source_target_pairs={{0,2},{2,0},{4,6},{6,4},{8,10},{10,8},{12,14},{14,12},{16,18},{18,... | collective-permute-start | bytes 442376 | tf_op jit(solution)/shard_map/ppermute | solution.py:170
  24.5 4.6 %collective-permute-start.3 = (f32[32,640]{1,0:T(8,128)S(1)}, f32[32,640]{1,0:T(8,128)S(1)}, u32[]{:S(2)}, u32[]{:S(2)}) collective-permute-start(f32[32,640]{1,0:T(8,128)S(1)} %pad_maximum_fusion.4), channel_id=1, source_target_pairs={{0,4},{2,6},{4,0},{6,2},{8,12},{10,14},{12,8},{14,10},{16,20},{18,... | collective-permute-start | bytes 245768 | tf_op jit(solution)/shard_map/ppermute | solution.py:170
  29.0 4.5 %collective-permute-start.4 = (f32[32,640]{1,0:T(8,128)S(1)}, f32[32,640]{1,0:T(8,128)S(1)}, u32[]{:S(2)}, u32[]{:S(2)}) collective-permute-start(f32[32,640]{1,0:T(8,128)S(1)} %fusion.3), channel_id=1, source_target_pairs={{0,8},{2,10},{4,12},{6,14},{8,0},{10,2},{12,4},{14,6},{16,24},{18,... | collective-permute-start | bytes 245768 | tf_op jit(solution)/shard_map/ppermute | solution.py:170
  33.6 5.4 %collective-permute-start.5 = (f32[32,640]{1,0:T(8,128)S(1)}, f32[32,640]{1,0:T(8,128)S(1)}, u32[]{:S(2)}, u32[]{:S(2)}) collective-permute-start(f32[32,640]{1,0:T(8,128)S(1)} %add.43), channel_id=1, source_target_pairs={{0,16},{2,18},{4,20},{6,22},{8,24},{10,26},{12,28},{14,30},{16,0},... | collective-permute-start | bytes 245768 | tf_op jit(solution)/shard_map/ppermute | solution.py:170
  36.2 14.0 %copy-start.2 = (f32[32,2048]{1,0:T(8,128)}, f32[32,2048]{1,0:T(8,128)S(1)}, u32[]{:S(2)}) copy-start(f32[32,2048]{1,0:T(8,128)S(1)} %constant_dynamic-update-slice_fusion) | copy-start | bytes 786436
  39.4 3.8 %collective-permute-start.8 = (f32[32,32]{1,0:T(8,128)S(1)}, f32[32,32]{1,0:T(8,128)S(1)}, u32[]{:S(2)}, u32[]{:S(2)}) collective-permute-start(f32[32,32]{1,0:T(8,128)S(1)} %fusion.16), channel_id=1, source_target_pairs={{0,1},{1,0},{2,3},{3,2},{4,5},{5,4},{6,7},{7,6},{8,9},{9,8},{10,11... | collective-permute-start | bytes 12296 | tf_op jit(solution)/shard_map/ppermute | solution.py:170
  39.8 4.6 %collective-permute-start.9 = (f32[32,32]{1,0:T(8,128)S(1)}, f32[32,32]{1,0:T(8,128)S(1)}, u32[]{:S(2)}, u32[]{:S(2)}) collective-permute-start(f32[32,32]{1,0:T(8,128)S(1)} %fusion.16), channel_id=1, source_target_pairs={{0,5},{1,4},{2,7},{3,6},{4,1},{5,0},{6,3},{7,2},{8,13},{9,12},{10,... | collective-permute-start | bytes 12296 | tf_op jit(solution)/shard_map/ppermute | solution.py:195
  42.4 4.5 %collective-permute-start.6 = (f32[32,640]{1,0:T(8,128)S(1)}, f32[32,640]{1,0:T(8,128)S(1)}, u32[]{:S(2)}, u32[]{:S(2)}) collective-permute-start(f32[32,640]{1,0:T(8,128)S(1)} %maximum_maximum_fusion), channel_id=1, source_target_pairs={{0,4},{2,6},{4,0},{6,2},{8,12},{10,14},{12,8},{14,10},{16,20},{18,... | collective-permute-start | bytes 245768 | tf_op jit(solution)/shard_map/ppermute | solution.py:170
  47.0 1.2 %collective-permute-start.10 = (f32[32,32]{1,0:T(8,128)S(1)}, f32[32,32]{1,0:T(8,128)S(1)}, u32[]{:S(2)}, u32[]{:S(2)}) collective-permute-start(f32[32,32]{1,0:T(8,128)S(1)} %slice_add_fusion), channel_id=1, source_target_pairs={{0,2},{2,0},{4,6},{6,4},{8,10},{10,8},{12,14},{14,12},{16,18},{18,... | collective-permute-start | bytes 12296 | tf_op jit(solution)/shard_map/ppermute | solution.py:170
  47.0 2.1 %collective-permute-start.7 = (f32[32,1024]{1,0:T(8,128)S(1)}, f32[32,1024]{1,0:T(8,128)S(1)}, u32[]{:S(2)}, u32[]{:S(2)}) collective-permute-start(f32[32,1024]{1,0:T(8,128)S(1)} %pad_maximum_fusion.3), channel_id=1, source_target_pairs={{0,2},{2,0},{4,6},{6,4},{8,10},{10,8},{12,14},{14,12},{16,18},{18,... | collective-permute-start | bytes 393224 | tf_op jit(solution)/shard_map/ppermute | solution.py:170
  49.2 1.1 %copy-start.1 = (f32[32,2048]{1,0:T(8,128)}, f32[32,2048]{1,0:T(8,128)S(1)}, u32[]{:S(2)}) copy-start(f32[32,2048]{1,0:T(8,128)S(1)} %pad_maximum_fusion) | copy-start | bytes 786436
